TPU v7x, 32 devices: a whole 2x2x4 slice. The times are simulated.
32 devices in a mesh: lat: 4 (over z), lon: 8 (over y, x, core).
Axes of the slice: x: 2, y: 2, z: 4, core: 2. Of those that a mesh axis runs over, the one named last changes fastest.
Arguments:
- state_grid: bfloat16 [24, 672, 192], P('lat', 'lon'), may hold values from -6 to 6
- norm_gain: float32 [192], replicated, may hold values from 0.1 to 1.9
- w_qkv: bfloat16 [192, 576], replicated, may hold values from -0.4375 to 0.4375
- w_proj: bfloat16 [192, 192], replicated, may hold values from -1.25 to 1.25
- bias_table: float32 [8, 6, 253], replicated, may hold values from -6 to 300
- window_kind: int32 [4, 56], replicated, may hold values from 0 to 7
- cotangent: bfloat16 [24, 672, 192], P('lat', 'lon'), may hold values from -6 to 6
Outputs:
- out_field: bfloat16 [24, 672, 192], P('lat', 'lon')
- d_field: bfloat16 [24, 672, 192], P('lat', 'lon')
- qkv_grad: float32 [192, 576], replicated
- proj_grad: float32 [192, 192], replicated
- table_grad: float32 [8, 6, 253], replicated
- gain_grad: float32 [192], replicated
All inputs are finite; a program needn't handle non-finite values.
Results may differ from a plain program's by a relative error of at most 0.009.
Values may be sent and summed in bfloat16 or wider, within the bound.
A program may use at most 64 MiB of HBM per device.

v0:
```python
import jax
import jax.numpy as jnp
from jax import lax
from jax.sharding import PartitionSpec as P

HEADS = 6
WIN_LAT = 6
WIN_LON = 12
norm_eps = 1e-05
clip_eps = 1e-06
clip_level = 1.0
masked_score = -1e30
highest = lax.Precision.HIGHEST


def shifted(value, axis, steps):
    count = lax.axis_size(axis)
    pairs = [(source, (source + steps) % count) for source in range(count)]
    return lax.ppermute(value, axis, pairs)


def relation_onehot(win_lat, win_lon):
    position = jnp.arange(win_lat * win_lon, dtype=jnp.int32)
    row_of = position // win_lon
    column = position % win_lon
    offset = (row_of[:, None] - row_of[None, :] + win_lat - 1) * (2 * win_lon - 1) + (
        column[:, None] - column[None, :] + win_lon - 1
    )
    extent = (2 * win_lat - 1) * (2 * win_lon - 1)
    return (offset.reshape(-1)[:, None] == jnp.arange(extent, dtype=jnp.int32)[None, :]).astype(
        jnp.float32
    )


def to_windows(source, win_lat, win_lon):
    rows_all, cols_all, channels = source.shape
    source = source.reshape(rows_all // win_lat, win_lat, cols_all // win_lon, win_lon, channels)
    return source.transpose(0, 2, 1, 3, 4).reshape(-1, win_lat * win_lon, channels)


def from_windows(windows, rows_all, cols_all, win_lat, win_lon):
    channels = windows.shape[-1]
    source = windows.reshape(rows_all // win_lat, cols_all // win_lon, win_lat, win_lon, channels)
    return source.transpose(0, 2, 1, 3, 4).reshape(rows_all, cols_all, channels)


def window_bias(bias_table, kinds_flat, onehot_rel, positions):
    kind_count, heads_n, extent = bias_table.shape
    spread = jnp.einsum(
        "ke,pe->kp",
        bias_table.reshape(kind_count * heads_n, extent),
        onehot_rel,
        precision=highest,
        preferred_element_type=jnp.float32,
    )
    kind_onehot = (kinds_flat[:, None] == jnp.arange(kind_count, dtype=jnp.int32)[None, :]).astype(
        jnp.float32
    )
    per_window = jnp.dot(
        kind_onehot,
        spread.reshape(kind_count, heads_n * positions * positions),
        precision=highest,
        preferred_element_type=jnp.float32,
    )
    return (per_window.reshape(-1, heads_n, positions, positions), kind_onehot)


def attend_forward(x_windows, norm_gain, w_qkv, w_proj, bias_win, allowed):
    count, positions, channels = x_windows.shape
    head_size = channels // HEADS
    inv_sqrt = head_size ** (-0.5)
    flat_rows = x_windows.reshape(-1, channels).astype(jnp.float32)
    centre = flat_rows - jnp.mean(flat_rows, axis=-1, keepdims=True)
    inverse = lax.rsqrt(jnp.mean(centre * centre, axis=-1, keepdims=True) + norm_eps)
    unit_rows = centre * inverse
    normed = (unit_rows * norm_gain).astype(jnp.bfloat16)
    qkv_rows = jnp.dot(normed, w_qkv, preferred_element_type=jnp.float32).astype(jnp.bfloat16)
    parts_qkv = qkv_rows.reshape(count, positions, 3, HEADS, head_size)
    queries = parts_qkv[:, :, 0]
    keys_in = parts_qkv[:, :, 1]
    values_in = parts_qkv[:, :, 2]
    scores = (
        jnp.einsum("wihd,wjhd->whij", queries, keys_in, preferred_element_type=jnp.float32)
        * inv_sqrt
        + bias_win
    )
    scores = jnp.where(allowed, scores, masked_score)
    soft_probs = jax.nn.softmax(scores, axis=-1)
    probs_low = soft_probs.astype(jnp.bfloat16)
    mixed_rows = jnp.einsum(
        "whij,wjhd->wihd", probs_low, values_in, preferred_element_type=jnp.float32
    )
    mixed_rows = mixed_rows.astype(jnp.bfloat16).reshape(-1, channels)
    branch = jnp.dot(mixed_rows, w_proj, preferred_element_type=jnp.float32).astype(jnp.bfloat16)
    saved = (
        normed,
        unit_rows,
        inverse,
        queries,
        keys_in,
        values_in,
        soft_probs,
        probs_low,
        mixed_rows,
    )
    return (saved, branch)


def attend_backward(
    saved, g_windows, keep_win, w_qkv, w_proj, norm_gain, kind_onehot, onehot_rel, table_dims
):
    normed, unit_rows, inverse, queries, keys_in, values_in, soft_probs, probs_low, mixed_rows = (
        saved
    )
    count, heads_n, positions = (soft_probs.shape[0], soft_probs.shape[1], soft_probs.shape[2])
    channels = normed.shape[1]
    head_size = channels // heads_n
    inv_sqrt = head_size ** (-0.5)
    flat_g = g_windows.reshape(-1, channels)
    keep_rows = keep_win.reshape(-1, 1)
    keep_low = keep_rows.astype(jnp.bfloat16)
    grad_proj = jnp.einsum(
        "nc,nd->cd", mixed_rows * keep_low, flat_g, preferred_element_type=jnp.float32
    )
    d_mixed = jnp.einsum("nd,cd->nc", flat_g, w_proj, preferred_element_type=jnp.float32).astype(
        jnp.bfloat16
    )
    d_mixed = d_mixed.reshape(count, positions, heads_n, head_size)
    d_probs = jnp.einsum("wihd,wjhd->whij", d_mixed, values_in, preferred_element_type=jnp.float32)
    d_values = jnp.einsum(
        "whij,wihd->wjhd", probs_low, d_mixed, preferred_element_type=jnp.float32
    ).astype(jnp.bfloat16)
    d_scores = soft_probs * (d_probs - jnp.sum(soft_probs * d_probs, axis=-1, keepdims=True))
    d_scores_low = d_scores.astype(jnp.bfloat16)
    d_queries = (
        jnp.einsum("whij,wjhd->wihd", d_scores_low, keys_in, preferred_element_type=jnp.float32)
        * inv_sqrt
    ).astype(jnp.bfloat16)
    d_keys = (
        jnp.einsum("whij,wihd->wjhd", d_scores_low, queries, preferred_element_type=jnp.float32)
        * inv_sqrt
    ).astype(jnp.bfloat16)
    d_qkv = jnp.stack([d_queries, d_keys, d_values], axis=2).reshape(-1, 3 * channels)
    grad_qkv = jnp.einsum("nc,nd->cd", normed * keep_low, d_qkv, preferred_element_type=jnp.float32)
    d_normed = jnp.einsum("nd,cd->nc", d_qkv, w_qkv, preferred_element_type=jnp.float32)
    grad_gain = jnp.sum(d_normed * unit_rows * keep_rows, axis=0)
    d_unit = d_normed * norm_gain
    d_path = inverse * (
        d_unit
        - jnp.mean(d_unit, axis=-1, keepdims=True)
        - unit_rows * jnp.mean(d_unit * unit_rows, axis=-1, keepdims=True)
    )
    d_path = d_path.astype(jnp.bfloat16)
    query_keep = keep_win.reshape(count, 1, positions, 1)
    by_kind = jnp.einsum(
        "wk,wx->kx",
        kind_onehot,
        (d_scores * query_keep).reshape(count, -1),
        precision=highest,
        preferred_element_type=jnp.float32,
    )
    grad_table = jnp.dot(
        by_kind.reshape(-1, positions * positions),
        onehot_rel,
        precision=highest,
        preferred_element_type=jnp.float32,
    )
    return (d_path, (grad_qkv, grad_proj, grad_table.reshape(table_dims), grad_gain))


def shifted_pair(source, half_lat, half_lon):
    upper = shifted(source[:half_lat], "lat", -1)
    stacked = jnp.concatenate([source[half_lat:], upper], axis=0)
    right_side = shifted(stacked[:, :half_lon], "lon", -1)
    return jnp.concatenate([stacked[:, half_lon:], right_side], axis=1)


def unshift_pair(block, half_lat, half_lon):
    trailing = shifted(block[:, -half_lon:], "lon", 1)
    placed = jnp.concatenate([trailing, block[:, :-half_lon]], axis=1)
    lower = shifted(placed[-half_lat:], "lat", 1)
    return jnp.concatenate([lower, placed[:-half_lat]], axis=0)


def clip_rms(gradient):
    return gradient * jnp.minimum(
        1.0, clip_level * lax.rsqrt(jnp.mean(gradient * gradient) + clip_eps)
    )


def on_device(state_grid, norm_gain, w_qkv, w_proj, bias_table, window_kind, cotangent):
    rows_dev, cols_dev, channels = state_grid.shape
    half_lat = WIN_LAT // 2
    half_lon = WIN_LON // 2
    positions = WIN_LAT * WIN_LON
    lat_index = lax.axis_index("lat")
    lon_index = lax.axis_index("lon")
    rows_all = rows_dev * lax.axis_size("lat")
    onehot_rel = relation_onehot(WIN_LAT, WIN_LON)
    band_start = lat_index * (rows_dev // WIN_LAT)
    sector_start = lon_index * (cols_dev // WIN_LON)
    first_row = lat_index * rows_dev + half_lat
    types_block = lax.dynamic_slice(
        window_kind, (band_start, sector_start), (rows_dev // WIN_LAT, cols_dev // WIN_LON)
    )
    keep_grid = jnp.ones((rows_dev, cols_dev), jnp.float32)
    joint = jnp.concatenate([state_grid, cotangent], axis=2)
    block_joint = shifted_pair(joint, half_lat, half_lon)
    block_x = block_joint[:, :, :channels]
    block_g = block_joint[:, :, channels:]
    block_rows, block_cols = (block_x.shape[0], block_x.shape[1])
    row_ids = (first_row + jnp.arange(block_rows, dtype=jnp.int32)) % rows_all
    labels = (row_ids + half_lat) // WIN_LAT
    label_grid = jnp.broadcast_to(labels[:, None, None], (block_rows, block_cols, 1))
    label_win = to_windows(label_grid, WIN_LAT, WIN_LON)[:, :, 0]
    allowed = (label_win[:, :, None] == label_win[:, None, :])[:, None]
    keep_win = to_windows(keep_grid[:, :, None], WIN_LAT, WIN_LON)[:, :, 0]
    bias_win, kind_onehot = window_bias(bias_table, types_block.reshape(-1), onehot_rel, positions)
    saved, branch = attend_forward(
        to_windows(block_x, WIN_LAT, WIN_LON), norm_gain, w_qkv, w_proj, bias_win, allowed
    )
    branch_grid = from_windows(
        branch.reshape(-1, positions, channels), block_rows, block_cols, WIN_LAT, WIN_LON
    )
    g_windows = to_windows(block_g, WIN_LAT, WIN_LON)
    d_path, grads = attend_backward(
        saved,
        g_windows,
        keep_win,
        w_qkv,
        w_proj,
        norm_gain,
        kind_onehot,
        onehot_rel,
        bias_table.shape,
    )
    path_grid = from_windows(
        d_path.reshape(-1, positions, channels), block_rows, block_cols, WIN_LAT, WIN_LON
    )
    both_own = unshift_pair(jnp.concatenate([branch_grid, path_grid], axis=2), half_lat, half_lon)
    branch_own = both_own[:, :, :channels]
    path_own = both_own[:, :, channels:]
    out_field = (state_grid.astype(jnp.float32) + branch_own.astype(jnp.float32)).astype(
        jnp.bfloat16
    )
    d_field = (cotangent.astype(jnp.float32) + path_own.astype(jnp.float32)).astype(jnp.bfloat16)
    grad_qkv, grad_proj, grad_table, grad_gain = grads
    summed = lax.psum((grad_qkv, grad_proj, grad_table, grad_gain), ("lat", "lon"))
    qkv_grad = clip_rms(summed[0])
    proj_grad = clip_rms(summed[1])
    table_grad = clip_rms(summed[2])
    gain_grad = clip_rms(summed[3])
    return (out_field, d_field, qkv_grad, proj_grad, table_grad, gain_grad)


def solution(mesh):
    in_specs = (P("lat", "lon", None), P(), P(), P(), P(), P(), P("lat", "lon", None))
    out_specs = (P("lat", "lon", None), P("lat", "lon", None), P(), P(), P(), P())
    return jax.shard_map(
        on_device, mesh=mesh, in_specs=in_specs, out_specs=out_specs, check_vma=False
    )
```

profile of v0, /device:TPU:1, one launch (start us, length us, event | category | flops | bytes accessed | tf_op | source)
XLA Modules:
  0.0 259.5 jit_solution(4553154303973583669)
XLA Ops:
  7.2 2.0 fusion.30
  9.2 4.1 %collective-permute-start = (bf16[3,84,384]{2,1,0:T(8,128)(2,1)}, bf16[3,84,384]{2,1,0:T(8,128)(2,1)S(1)}, u32[]{:S(2)}, u32[]{:S(2)}) collective-permute-start(bf16[3,84,384]{2,1,0:T(8,128)(2,1)} %get-tuple-element.17), channel_id=1, source_target_pairs={{0,24},{8,0},{16,8},{24,16},{1,25},{9,1},{17,9},{25,17},{2,26},{10... | collective-permute-start | bytes 580616 | tf_op jit(solution)/shard_map/ppermute | solution.py:19
  13.7 0.8 copy.58
  14.6 2.6 %convolution_bitcast_fusion = f32[48,5184]{1,0:T(8,128)S(1)} fusion(f32[48,253]{1,0:T(8,128)S(1)} %reshape.225, s32[5184]{0:T(1024)S(1)} %add.155), kind=kOutput, calls=%fused_computation.1 | convolution fusion | flops 756765504 | bytes 1064640 | tf_op jit(solution)/shard_map/ke,pe->kp/dot_general | solution.py:49
  17.2 0.7 reshape.226
  17.9 2.7 %dot_general.63 = f32[6,72,72,8]{2,1,0,3:T(8,128)} reshape(f32[31104,8]{0,1:T(8,128)S(1)} %bitcast.82) | data formatting | bytes 1990656 | tf_op jit(solution)/shard_map/dot_general | solution.py:59
  20.6 0.8 dynamic-slice_bitcast_fusion
  21.4 2.8 %fusion.6 = f32[7,6,72,72]{3,0,2,1:T(8,128)S(1)} fusion(f32[6,72,72,8]{2,1,0,3:T(8,128)} %dot_general.63, s32[7]{0:T(128)S(1)} %dynamic-slice_bitcast_fusion), kind=kOutput, calls=%fused_computation.7 | convolution fusion | flops 20901944 | bytes 1866268 | tf_op jit(solution)/shard_map/dot_general | solution.py:59
  24.2 1.6 copy.61
  25.9 1.0 collective-permute-start.1
  27.1 2.6 %collective-permute-done.1 = bf16[6,6,384]{2,1,0:T(8,128)(2,1)S(1)} collective-permute-done((bf16[6,6,384]{2,1,0:T(8,128)(2,1)S(1)}, bf16[6,6,384]{2,1,0:T(8,128)(2,1)S(1)}, u32[]{:S(2)}, u32[]{:S(2)}) %collective-permute-start.1) | collective-permute-done | bytes 27680 | tf_op jit(solution)/shard_map/ppermute | solution.py:19
  30.7 1.0 multiply_convert_fusion
  31.8 0.8 reshape_reshape.11
  33.0 0.7 copy-done.3
  34.1 1.0 reshape.224
  35.1 0.8 fusion.41
  36.0 0.7 copy-done.5
  37.3 2.3 fusion.43
  39.7 2.3 fusion.12
  42.0 1.9 copy.63
  43.9 1.3 reshape.227
  45.2 1.9 convolution_convert_fusion.3
  47.2 1.9 fusion.45
  49.0 1.8 convolution_convert_fusion.4
  50.9 2.0 reshape.230
  52.9 2.3 fusion.13
  55.2 1.8 multiply_reduce_fusion
  57.9 1.3 fusion.14
  59.2 1.1 fusion.15
  60.7 1.0 copy.75
  61.8 0.8 convert_element_type.116
  62.9 0.8 reshape.228
  63.7 2.2 reshape.233
  66.1 0.7 copy.72
  66.8 0.7 reshape.231
  68.1 0.7 fusion.16
  68.8 1.9 fusion.2
  71.2 1.2 fusion.44
  72.4 36.5 %all-reduce = (f32[8,6,253]{2,0,1:T(8,128)S(1)}, f32[192]{0:T(256)S(1)}) all-reduce(f32[8,6,253]{2,0,1:T(8,128)S(1)} %fusion.2, f32[192]{0:T(256)S(1)} %get-tuple-element.6), channel_id=1, replica_groups=mesh['lat'=4,'lon'=8] {'lat','lon'}, use_global_device_ids=true, to_apply=%region_11.12 | all-reduce | flops 12336 | bytes 98688 | tf_op jit(solution)/shard_map/psum | solution.py:248
  111.9 3.4 %collective-permute-start.2 = (bf16[6,6,384]{2,1,0:T(8,128)(2,1)S(1)}, bf16[6,6,384]{2,1,0:T(8,128)(2,1)S(1)}, u32[]{:S(2)}, u32[]{:S(2)}) collective-permute-start(bf16[6,6,384]{2,1,0:T(8,128)(2,1)S(1)} %pad_maximum_fusion.5), channel_id=1, source_target_pairs={{0,1},{1,2},{2,3},{3,4},{4,5},{5,6},{6,7},{7,0},{8,9},{9,10},{10,1... | collective-permute-start | bytes 82952 | tf_op jit(solution)/shard_map/ppermute | solution.py:19
  116.8 2.5 collective-permute-start.3
  119.9 4.2 %collective-permute-done.3 = bf16[3,84,384]{2,1,0:T(8,128)(2,1)S(1)} collective-permute-done((bf16[3,84,384]{2,1,0:T(8,128)(2,1)S(1)}, bf16[3,84,384]{2,1,0:T(8,128)(2,1)S(1)}, u32[]{:S(2)}, u32[]{:S(2)}) %collective-permute-start.3) | collective-permute-done | bytes 193568 | tf_op jit(solution)/shard_map/ppermute | solution.py:19
  124.1 1.0 add_convert_fusion
  125.1 120.2 %all-reduce.4.cloned.1.call-done = (f32[192,576]{1,0:T(8,128)}, f32[192,192]{1,0:T(8,128)}) async-done(((f32[192,576]{1,0:T(8,128)}, f32[192,192]{1,0:T(8,128)}), (f32[192,576]{1,0:T(8,128)}, f32[192,192]{1,0:T(8,128)})) %all-reduce.4.cloned.1.call-update) | async-done | bytes 589840 | tf_op jit(solution)/shard_map/psum | solution.py:248
  245.3 1.7 multiply_reduce_fusion.6
  247.6 1.8 multiply_reduce_fusion.2
  250.1 1.8 broadcast_multiply_fusion
  251.9 0.7 broadcast_multiply_fusion.1
  (97 shorter events, 9.6 us)
Async XLA Ops:
  7.2 26.5 %copy-start = (bf16[192,576]{1,0:T(8,128)(2,1)S(1)}, bf16[192,576]{1,0:T(8,128)(2,1)}, u32[]{:S(2)}) copy-start(bf16[192,576]{1,0:T(8,128)(2,1)} %param.9) | copy-start | bytes 663556
  7.2 238.1 %all-reduce.4.cloned.1.call-start = ((), (), s32[]{:S(2)}) async-start(), calls=%async_computation | async-start | bytes 1376256 | tf_op jit(solution)/shard_map/psum | solution.py:248
  9.2 16.7 %collective-permute-start = (bf16[3,84,384]{2,1,0:T(8,128)(2,1)}, bf16[3,84,384]{2,1,0:T(8,128)(2,1)S(1)}, u32[]{:S(2)}, u32[]{:S(2)}) collective-permute-start(bf16[3,84,384]{2,1,0:T(8,128)(2,1)} %get-tuple-element.17), channel_id=1, source_target_pairs={{0,24},{8,0},{16,8},{24,16},{1,25},{9,1},{17,9},{25,17},{2,26},{10... | collective-permute-start | bytes 580616 | tf_op jit(solution)/shard_map/ppermute | solution.py:19
  13.7 0.9 copy-start.20
  25.9 3.7 %collective-permute-start.1 = (bf16[6,6,384]{2,1,0:T(8,128)(2,1)S(1)}, bf16[6,6,384]{2,1,0:T(8,128)(2,1)S(1)}, u32[]{:S(2)}, u32[]{:S(2)}) collective-permute-start(bf16[6,6,384]{2,1,0:T(8,128)(2,1)S(1)} %pad_maximum_fusion.6), channel_id=1, source_target_pairs={{0,7},{1,0},{2,1},{3,2},{4,3},{5,4},{6,5},{7,6},{8,15},{9,8},{10,9... | collective-permute-start | bytes 82952 | tf_op jit(solution)/shard_map/ppermute | solution.py:19
  29.9 0.8 copy-start.22
  33.0 0.7 copy-start.3
  35.1 1.6 copy-start.1
  36.0 0.7 copy-start.5
  36.0 1.4 copy-start.7
  39.7 2.3 copy-start.18
  52.9 2.3 copy-start.19
  56.9 1.0 copy-start.8
  57.9 1.3 copy-start.6
  60.3 2.3 copy-start.16
  62.8 3.0 %copy-start.10 = (bf16[7,72,1,6,32]{1,4,3,0,2:T(8,128)(2,1)S(1)}, bf16[7,72,1,6,32]{1,4,3,0,2:T(8,128)(2,1)}, u32[]{:S(2)}) copy-start(bf16[7,72,1,6,32]{1,4,3,0,2:T(8,128)(2,1)} %fusion.14) | copy-start | bytes 580612
  62.9 3.0 %copy-start.11 = (bf16[7,72,1,6,32]{1,4,3,0,2:T(8,128)(2,1)S(1)}, bf16[7,72,1,6,32]{1,4,3,0,2:T(8,128)(2,1)}, u32[]{:S(2)}) copy-start(bf16[7,72,1,6,32]{1,4,3,0,2:T(8,128)(2,1)} %fusion.15) | copy-start | bytes 580612
  62.9 3.0 %copy-start.17 = (bf16[7,72,1,6,32]{1,4,3,0,2:T(8,128)(2,1)S(1)}, bf16[7,72,1,6,32]{1,4,3,0,2:T(8,128)(2,1)}, u32[]{:S(2)}) copy-start(bf16[7,72,1,6,32]{1,4,3,0,2:T(8,128)(2,1)} %fusion.13) | copy-start | bytes 580612
  66.1 1.5 copy-start.2
  68.1 0.7 copy-start.21
  68.1 2.6 %copy-start.4 = (f32[504,192]{0,1:T(8,128)S(1)}, f32[504,192]{0,1:T(8,128)}, u32[]{:S(2)}) copy-start(f32[504,192]{0,1:T(8,128)} %copy-done.3) | copy-start | bytes 1161220
  68.8 2.4 copy-start.14
  110.8 1.0 copy-start.9
  111.8 12.4 %copy-start.12 = (bf16[6,84,192]{2,1,0:T(8,128)(2,1)S(1)}, bf16[6,84,192]{2,1,0:T(8,128)(2,1)}, u32[]{:S(2)}) copy-start(bf16[6,84,192]{2,1,0:T(8,128)(2,1)} %param.13) | copy-start | bytes 580612
  111.8 12.4 %copy-start.13 = (bf16[6,84,192]{2,1,0:T(8,128)(2,1)S(1)}, bf16[6,84,192]{2,1,0:T(8,128)(2,1)}, u32[]{:S(2)}) copy-start(bf16[6,84,192]{2,1,0:T(8,128)(2,1)} %param.7) | copy-start | bytes 580612
  111.9 4.7 %collective-permute-start.2 = (bf16[6,6,384]{2,1,0:T(8,128)(2,1)S(1)}, bf16[6,6,384]{2,1,0:T(8,128)(2,1)S(1)}, u32[]{:S(2)}, u32[]{:S(2)}) collective-permute-start(bf16[6,6,384]{2,1,0:T(8,128)(2,1)S(1)} %pad_maximum_fusion.5), channel_id=1, source_target_pairs={{0,1},{1,2},{2,3},{3,4},{4,5},{5,6},{6,7},{7,0},{8,9},{9,10},{10,1... | collective-permute-start | bytes 82952 | tf_op jit(solution)/shard_map/ppermute | solution.py:19
  116.8 7.3 %collective-permute-start.3 = (bf16[3,84,384]{2,1,0:T(8,128)(2,1)S(1)}, bf16[3,84,384]{2,1,0:T(8,128)(2,1)S(1)}, u32[]{:S(2)}, u32[]{:S(2)}) collective-permute-start(bf16[3,84,384]{2,1,0:T(8,128)(2,1)S(1)} %get-tuple-element.21), channel_id=1, source_target_pairs={{0,8},{8,16},{16,24},{24,0},{1,9},{9,17},{17,25},{25,1},{2,10},{10... | collective-permute-start | bytes 580616 | tf_op jit(solution)/shard_map/ppermute | solution.py:19
  245.3 6.6 %copy-start.15 = (f32[192,192]{1,0:T(8,128)S(1)}, f32[192,192]{1,0:T(8,128)}, u32[]{:S(2)}) copy-start(f32[192,192]{1,0:T(8,128)} %get-tuple-element.12) | copy-start | bytes 442372
Sparse Core Ops, SparseCore 0:
  116.7 128.5 all-reduce.3
where the time goes:
time: 260 us; the launch traced here: 259 us
  waiting for transfers between devices  127 us (49%)
  blocking collectives  36.5 us (14%)
  local copies, waits for them, and re-layouts  26 us (10%)
  matrix products  25 us (10%)
  between operations  17.3 us (7%)
  other arithmetic  16.6 us (6%)
  starting transfers between devices  11.1 us (4%)
    psum x1, waiting for transfers between devices, on_device(): lax.psum((grad_qkv, grad_proj, grad_table, grad_gain), ('lat', 'lon'))  120 us
    psum x1, blocking collectives, on_device(): lax.psum((grad_qkv, grad_proj, grad_table, grad_gain), ('lat', 'lon'))  36.5 us
    ppermute x4, starting transfers between devices, shifted(): return lax.ppermute(value, axis, pairs)  11.1 us
    ppermute x4, waiting for transfers between devices, shifted(): return lax.ppermute(value, axis, pairs)  6.82 us
  transfers between devices with their start and end apart: 5, of which 3 were waited for; matrix products, arithmetic and copies ran while one was open for 6% of the time, Pallas kernels for 0%

commit v1 on v0

--- a/solution.py
+++ b/solution.py
@@ -245,7 +245,8 @@
     )
     d_field = (cotangent.astype(jnp.float32) + path_own.astype(jnp.float32)).astype(jnp.bfloat16)
     grad_qkv, grad_proj, grad_table, grad_gain = grads
-    summed = lax.psum((grad_qkv, grad_proj, grad_table, grad_gain), ("lat", "lon"))
+    one_axis = lax.psum((grad_qkv, grad_proj, grad_table, grad_gain), "lon")
+    summed = lax.psum(one_axis, "lat")
     qkv_grad = clip_rms(summed[0])
     proj_grad = clip_rms(summed[1])
     table_grad = clip_rms(summed[2])

time: 260 us -> 228 us (0.88)
  waiting for transfers between devices: 127 us -> 94.3 us
    psum x1 -> x2, waiting for transfers between devices: 120 us -> 85.4 us  [the longest x1 49.9 us: on_device(): one_axis = lax.psum((grad_qkv, grad_proj, grad_table, grad_gain), 'lon')]
    psum x1 -> x2, blocking collectives: 36.5 us -> 35.7 us  [the longest x1 22.6 us: on_device(): one_axis = lax.psum((grad_qkv, grad_proj, grad_table, grad_gain), 'lon')]
  transfers between devices with their start and end apart: 5 -> 6, of which waited for: 3 -> 5; matrix products, arithmetic and copies ran while one was open for 6% -> 7% of each run, Pallas kernels for 0% -> 0%
where the time goes in v1:
time: 228 us; the launch traced here: 226 us
  waiting for transfers between devices  94.3 us (41%)
  blocking collectives  35.7 us (16%)
  local copies, waits for them, and re-layouts  25.9 us (11%)
  matrix products  25 us (11%)
  between operations  17.4 us (8%)
  other arithmetic  16 us (7%)
  starting transfers between devices  11.8 us (5%)
    psum x1, waiting for transfers between devices, on_device(): one_axis = lax.psum((grad_qkv, grad_proj, grad_table, grad_gain), 'lon')  49.9 us
    psum x1, waiting for transfers between devices, on_device(): summed = lax.psum(one_axis, 'lat')  35.5 us
    psum x1, blocking collectives, on_device(): one_axis = lax.psum((grad_qkv, grad_proj, grad_table, grad_gain), 'lon')  22.6 us
    psum x1, blocking collectives, on_device(): summed = lax.psum(one_axis, 'lat')  13.2 us
    ppermute x4, starting transfers between devices, shifted(): return lax.ppermute(value, axis, pairs)  11.7 us
    ppermute x4, waiting for transfers between devices, shifted(): return lax.ppermute(value, axis, pairs)  8.91 us
    reduce_sum x4, other arithmetic, clip_rms(): jnp.mean(gradient * gradient) + clip_eps  4.62 us
  transfers between devices with their start and end apart: 6, of which 5 were waited for; matrix products, arithmetic and copies ran while one was open for 7% of the time, Pallas kernels for 0%

profile of v1, /device:TPU:1, one launch (start us, length us, event | category | flops | bytes accessed | tf_op | source)
XLA Modules:
  0.0 226.2 jit_solution(11307566781013489508)
XLA Ops:
  7.2 1.3 fusion.30
  8.5 4.2 %collective-permute-start = (bf16[3,84,384]{2,1,0:T(8,128)(2,1)S(1)}, bf16[3,84,384]{2,1,0:T(8,128)(2,1)S(1)}, u32[]{:S(2)}, u32[]{:S(2)}) collective-permute-start(bf16[3,84,384]{2,1,0:T(8,128)(2,1)S(1)} %get-tuple-element.21), channel_id=1, source_target_pairs={{0,24},{8,0},{16,8},{24,16},{1,25},{9,1},{17,9},{25,17},{2,26},{10... | collective-permute-start | bytes 580616 | tf_op jit(solution)/shard_map/ppermute | solution.py:19
  13.1 0.8 copy.58
  14.0 2.6 %convolution_bitcast_fusion = f32[48,5184]{1,0:T(8,128)S(1)} fusion(f32[48,253]{1,0:T(8,128)S(1)} %reshape.225, s32[5184]{0:T(1024)S(1)} %add.163), kind=kOutput, calls=%fused_computation.1 | convolution fusion | flops 756765504 | bytes 1064640 | tf_op jit(solution)/shard_map/ke,pe->kp/dot_general | solution.py:49
  16.6 0.7 reshape.226
  17.3 2.7 %dot_general.63 = f32[6,72,72,8]{2,1,0,3:T(8,128)} reshape(f32[31104,8]{0,1:T(8,128)S(1)} %bitcast.82) | data formatting | bytes 1990656 | tf_op jit(solution)/shard_map/dot_general | solution.py:59
  20.0 0.8 dynamic-slice_bitcast_fusion
  20.8 2.8 %fusion.6 = f32[7,6,72,72]{3,0,2,1:T(8,128)S(1)} fusion(f32[6,72,72,8]{2,1,0,3:T(8,128)} %dot_general.63, s32[7]{0:T(128)S(1)} %dynamic-slice_bitcast_fusion), kind=kOutput, calls=%fused_computation.7 | convolution fusion | flops 20901944 | bytes 1866268 | tf_op jit(solution)/shard_map/dot_general | solution.py:59
  23.6 1.6 copy.61
  25.4 1.0 collective-permute-start.1
  26.5 2.6 %collective-permute-done.1 = bf16[6,6,384]{2,1,0:T(8,128)(2,1)S(1)} collective-permute-done((bf16[6,6,384]{2,1,0:T(8,128)(2,1)S(1)}, bf16[6,6,384]{2,1,0:T(8,128)(2,1)S(1)}, u32[]{:S(2)}, u32[]{:S(2)}) %collective-permute-start.1) | collective-permute-done | bytes 27680 | tf_op jit(solution)/shard_map/ppermute | solution.py:19
  30.1 1.0 multiply_convert_fusion
  31.2 0.8 reshape_reshape.11
  32.4 0.7 copy-done.3
  33.5 1.0 reshape.224
  34.6 0.8 fusion.41
  35.4 0.7 copy-done.5
  36.8 2.3 %fusion.43 = (f32[7,6,72]{2,1,0:T(8,128)S(1)}, f32[7,6,72,72]{2,3,1,0:T(8,128)S(1)}) fusion(f32[7,6,72,72]{2,3,1,0:T(8,128)S(1)} %add_select_fusion), kind=kOutput, calls=%fused_computation.105 | output fusion | flops 435527 | bytes 1753920 | tf_op jit(solution)/shard_map/sub | solution.py:88
  39.1 2.3 %fusion.12 = bf16[7,72,6,32]{1,3,2,0:T(8,128)(2,1)} fusion(bf16[7,72,1,6,32]{1,0,4,3,2:T(8,128)(2,1)} %get-tuple-element.17, f32[7,6,72]{2,1,0:T(8,128)S(1)} %get-tuple-element.28, f32[7,6,72,72]{2,3,1,0:T(8,128)S(1)} %add_select_fusion), kind=kOutput, calls=%fused_computation.21 | convolution fusion | flops 14687639 | bytes 1270080 | tf_op jit(solution)/shard_map/whij,wjhd->wihd/dot_general | solution.py:90
  41.4 1.9 copy.63
  43.4 1.3 reshape.227
  44.7 1.9 convolution_convert_fusion.3
  46.6 1.9 fusion.45
  48.5 1.8 convolution_convert_fusion.4
  50.3 2.0 reshape.230
  52.3 2.3 %fusion.13 = bf16[7,72,1,6,32]{1,4,3,0,2:T(8,128)(2,1)} fusion(bf16[7,72,6,32]{1,0,3,2:T(8,128)(2,1)} %reshape.230, f32[7,6,72]{2,1,0:T(8,128)} %copy-done.18, f32[7,6,72,72]{2,3,1,0:T(8,128)S(1)} %add_select_fusion), kind=kOutput, calls=%fused_computation.22 | convolution fusion | flops 14687639 | bytes 1270080 | tf_op jit(solution)/shard_map/whij,wihd->wjhd/dot_general | solution.py:130
  54.6 1.7 multiply_reduce_fusion
  57.4 1.3 fusion.14
  58.6 1.1 fusion.15
  60.2 1.0 copy.75
  61.2 0.8 convert_element_type.116
  62.3 0.8 reshape.228
  63.1 2.2 reshape.233
  66.3 0.7 reshape.231
  68.2 1.9 fusion.2
  70.6 1.2 fusion.44
  71.8 22.6 %all-reduce = (f32[8,6,253]{2,0,1:T(8,128)S(1)}, f32[192]{0:T(256)S(1)}) all-reduce(f32[8,6,253]{2,0,1:T(8,128)S(1)} %fusion.2, f32[192]{0:T(256)S(1)} %get-tuple-element.6), channel_id=1, replica_groups=mesh['lat'=4,'lon'=8] {'lon'}, use_global_device_ids=true, to_apply=%region_13.14 | all-reduce | flops 12336 | bytes 98688 | tf_op jit(solution)/shard_map/psum | solution.py:248
  94.4 13.2 %all-reduce.2 = (f32[8,6,253]{2,0,1:T(8,128)S(1)}, f32[192]{0:T(256)S(1)}) all-reduce(f32[8,6,253]{2,0,1:T(8,128)S(1)} %get-tuple-element.9, f32[192]{0:T(256)S(1)} %get-tuple-element.10), channel_id=1, replica_groups=mesh['lat'=4,'lon'=8] {'lat'}, use_global_device_ids=true, to_apply=%region_14.15 | all-reduce | flops 12336 | bytes 98688 | tf_op jit(solution)/shard_map/psum | solution.py:249
  110.7 5.3 %collective-permute-start.2 = (bf16[6,6,384]{2,1,0:T(8,128)(2,1)S(1)}, bf16[6,6,384]{2,1,0:T(8,128)(2,1)S(1)}, u32[]{:S(2)}, u32[]{:S(2)}) collective-permute-start(bf16[6,6,384]{2,1,0:T(8,128)(2,1)S(1)} %pad_maximum_fusion.5), channel_id=1, source_target_pairs={{0,1},{1,2},{2,3},{3,4},{4,5},{5,6},{6,7},{7,0},{8,9},{9,10},{10,1... | collective-permute-start | bytes 82952 | tf_op jit(solution)/shard_map/ppermute | solution.py:19
  117.2 1.1 collective-permute-done.2
  118.5 49.9 %all-reduce.7.cloned.1.call-done = (f32[192,576]{1,0:T(8,128)}, f32[192,192]{1,0:T(8,128)}) async-done(((f32[192,576]{1,0:T(8,128)}, f32[192,192]{1,0:T(8,128)}), (f32[192,576]{1,0:T(8,128)}, f32[192,192]{1,0:T(8,128)})) %all-reduce.7.cloned.1.call-update) | async-done | bytes 589840 | tf_op jit(solution)/shard_map/psum | solution.py:248
  168.5 1.3 collective-permute-start.3
  170.3 5.2 %collective-permute-done.3 = bf16[3,84,384]{2,1,0:T(8,128)(2,1)S(1)} collective-permute-done((bf16[3,84,384]{2,1,0:T(8,128)(2,1)S(1)}, bf16[3,84,384]{2,1,0:T(8,128)(2,1)S(1)}, u32[]{:S(2)}, u32[]{:S(2)}) %collective-permute-start.3) | collective-permute-done | bytes 193568 | tf_op jit(solution)/shard_map/ppermute | solution.py:19
  175.5 1.0 add_convert_fusion
  176.5 35.5 %all-reduce.9.cloned.1.call-done = (f32[192,576]{1,0:T(8,128)}, f32[192,192]{1,0:T(8,128)}) async-done(((f32[192,576]{1,0:T(8,128)}, f32[192,192]{1,0:T(8,128)}), (f32[192,576]{1,0:T(8,128)}, f32[192,192]{1,0:T(8,128)})) %all-reduce.9.cloned.1.call-update) | async-done | bytes 589840 | tf_op jit(solution)/shard_map/psum | solution.py:249
  212.0 1.7 multiply_reduce_fusion.6
  214.3 1.8 multiply_reduce_fusion.2
  216.8 1.8 broadcast_multiply_fusion
  (101 shorter events, 11.8 us)
Async XLA Ops:
  7.2 26.0 %copy-start = (bf16[192,576]{1,0:T(8,128)(2,1)S(1)}, bf16[192,576]{1,0:T(8,128)(2,1)}, u32[]{:S(2)}) copy-start(bf16[192,576]{1,0:T(8,128)(2,1)} %param.9) | copy-start | bytes 663556
  7.2 161.2 %all-reduce.7.cloned.1.call-start = ((), (), s32[]{:S(2)}) async-start(), calls=%async_computation | async-start | bytes 1376256 | tf_op jit(solution)/shard_map/psum | solution.py:248
  8.5 16.8 %collective-permute-start = (bf16[3,84,384]{2,1,0:T(8,128)(2,1)S(1)}, bf16[3,84,384]{2,1,0:T(8,128)(2,1)S(1)}, u32[]{:S(2)}, u32[]{:S(2)}) collective-permute-start(bf16[3,84,384]{2,1,0:T(8,128)(2,1)S(1)} %get-tuple-element.21), channel_id=1, source_target_pairs={{0,24},{8,0},{16,8},{24,16},{1,25},{9,1},{17,9},{25,17},{2,26},{10... | collective-permute-start | bytes 580616 | tf_op jit(solution)/shard_map/ppermute | solution.py:19
  13.1 0.9 copy-start.20
  25.4 3.7 %collective-permute-start.1 = (bf16[6,6,384]{2,1,0:T(8,128)(2,1)S(1)}, bf16[6,6,384]{2,1,0:T(8,128)(2,1)S(1)}, u32[]{:S(2)}, u32[]{:S(2)}) collective-permute-start(bf16[6,6,384]{2,1,0:T(8,128)(2,1)S(1)} %pad_maximum_fusion.6), channel_id=1, source_target_pairs={{0,7},{1,0},{2,1},{3,2},{4,3},{5,4},{6,5},{7,6},{8,15},{9,8},{10,9... | collective-permute-start | bytes 82952 | tf_op jit(solution)/shard_map/ppermute | solution.py:19
  29.3 0.8 copy-start.22
  32.4 0.7 copy-start.3
  34.5 1.6 copy-start.1
  35.4 0.7 copy-start.5
  35.4 1.4 copy-start.7
  39.1 2.3 %copy-start.18 = (f32[7,6,72]{2,1,0:T(8,128)}, f32[7,6,72]{2,1,0:T(8,128)S(1)}, u32[]{:S(2)}) copy-start(f32[7,6,72]{2,1,0:T(8,128)S(1)} %get-tuple-element.28) | copy-start | bytes 36292
  52.3 2.3 %copy-start.19 = (f32[7,6,72]{2,1,0:T(8,128)S(1)}, f32[7,6,72]{2,1,0:T(8,128)}, u32[]{:S(2)}) copy-start(f32[7,6,72]{2,1,0:T(8,128)} %copy-done.18) | copy-start | bytes 36292
  56.4 1.0 copy-start.8
  57.4 1.3 copy-start.6
  59.7 2.3 %copy-start.16 = (bf16[504,192]{0,1:T(8,128)(2,1)S(1)}, bf16[504,192]{0,1:T(8,128)(2,1)}, u32[]{:S(2)}) copy-start(bf16[504,192]{0,1:T(8,128)(2,1)} %convolution_convert_fusion.4) | copy-start | bytes 580612
  62.3 3.0 %copy-start.10 = (bf16[7,72,1,6,32]{1,4,3,0,2:T(8,128)(2,1)S(1)}, bf16[7,72,1,6,32]{1,4,3,0,2:T(8,128)(2,1)}, u32[]{:S(2)}) copy-start(bf16[7,72,1,6,32]{1,4,3,0,2:T(8,128)(2,1)} %fusion.14) | copy-start | bytes 580612
  62.3 3.0 %copy-start.11 = (bf16[7,72,1,6,32]{1,4,3,0,2:T(8,128)(2,1)S(1)}, bf16[7,72,1,6,32]{1,4,3,0,2:T(8,128)(2,1)}, u32[]{:S(2)}) copy-start(bf16[7,72,1,6,32]{1,4,3,0,2:T(8,128)(2,1)} %fusion.15) | copy-start | bytes 580612
  62.3 3.0 %copy-start.17 = (bf16[7,72,1,6,32]{1,4,3,0,2:T(8,128)(2,1)S(1)}, bf16[7,72,1,6,32]{1,4,3,0,2:T(8,128)(2,1)}, u32[]{:S(2)}) copy-start(bf16[7,72,1,6,32]{1,4,3,0,2:T(8,128)(2,1)} %fusion.13) | copy-start | bytes 580612
  65.6 1.4 copy-start.2
  67.5 0.7 copy-start.21
  67.5 2.6 %copy-start.4 = (f32[504,192]{0,1:T(8,128)S(1)}, f32[504,192]{0,1:T(8,128)}, u32[]{:S(2)}) copy-start(f32[504,192]{0,1:T(8,128)} %copy-done.3) | copy-start | bytes 1161220
  68.2 2.4 %copy-start.14 = (bf16[504,192]{1,0:T(8,128)(2,1)S(1)}, bf16[504,192]{1,0:T(8,128)(2,1)}, u32[]{:S(2)}) copy-start(bf16[504,192]{1,0:T(8,128)(2,1)} %convert_element_type.116) | copy-start | bytes 580612
  109.6 1.0 copy-start.9
  110.0 65.5 %copy-start.12 = (bf16[6,84,192]{2,1,0:T(8,128)(2,1)S(1)}, bf16[6,84,192]{2,1,0:T(8,128)(2,1)}, u32[]{:S(2)}) copy-start(bf16[6,84,192]{2,1,0:T(8,128)(2,1)} %param.13) | copy-start | bytes 580612
  110.1 65.5 %copy-start.13 = (bf16[6,84,192]{2,1,0:T(8,128)(2,1)S(1)}, bf16[6,84,192]{2,1,0:T(8,128)(2,1)}, u32[]{:S(2)}) copy-start(bf16[6,84,192]{2,1,0:T(8,128)(2,1)} %param.7) | copy-start | bytes 580612
  110.1 101.9 %all-reduce.9.cloned.1.call-start = ((), (), s32[]{:S(2)}) async-start(), calls=%async_computation.1 | async-start | bytes 1376256 | tf_op jit(solution)/shard_map/psum | solution.py:249
  110.7 7.6 %collective-permute-start.2 = (bf16[6,6,384]{2,1,0:T(8,128)(2,1)S(1)}, bf16[6,6,384]{2,1,0:T(8,128)(2,1)S(1)}, u32[]{:S(2)}, u32[]{:S(2)}) collective-permute-start(bf16[6,6,384]{2,1,0:T(8,128)(2,1)S(1)} %pad_maximum_fusion.5), channel_id=1, source_target_pairs={{0,1},{1,2},{2,3},{3,4},{4,5},{5,6},{6,7},{7,0},{8,9},{9,10},{10,1... | collective-permute-start | bytes 82952 | tf_op jit(solution)/shard_map/ppermute | solution.py:19
  168.5 7.0 %collective-permute-start.3 = (bf16[3,84,384]{2,1,0:T(8,128)(2,1)S(1)}, bf16[3,84,384]{2,1,0:T(8,128)(2,1)S(1)}, u32[]{:S(2)}, u32[]{:S(2)}) collective-permute-start(bf16[3,84,384]{2,1,0:T(8,128)(2,1)S(1)} %get-tuple-element.25), channel_id=1, source_target_pairs={{0,8},{8,16},{16,24},{24,0},{1,9},{9,17},{17,25},{25,1},{2,10},{10... | collective-permute-start | bytes 580616 | tf_op jit(solution)/shard_map/ppermute | solution.py:19
  212.0 6.6 %copy-start.15 = (f32[192,192]{1,0:T(8,128)S(1)}, f32[192,192]{1,0:T(8,128)}, u32[]{:S(2)}) copy-start(f32[192,192]{1,0:T(8,128)} %get-tuple-element.16) | copy-start | bytes 442372
Sparse Core Ops, SparseCore 0:
  110.2 58.2 all-reduce.6
  170.8 41.0 all-reduce.8
